TPU v7x, 32 devices: a whole 2x2x4 slice. The times are simulated.
32 devices in a mesh: dp: 4 (over y, x), atom: 8 (over z, core).
Axes of the slice: x: 2, y: 2, z: 4, core: 2. Of those that a mesh axis runs over, the one named last changes fastest.
Arguments:
- patch_slots: bfloat16 [4, 768, 1024], P('dp', 'atom'), may hold values from -6 to 6
- slot_counts: int32 [4, 8], P('dp'), may hold values from 1 to 96, 256 in all within a row
- dictionary: bfloat16 [1024, 8192], P(None, 'atom')
Outputs:
- sparse_codes: float32 [4, 256, 8192], P('dp', None, 'atom')
- new_dictionary: float32 [1024, 8192], P('dp', 'atom')
Inputs may be any that keep to these rules, and one draw needn't show every extreme that they name: `slot_counts`: each row sums to 256 and its largest entry is exactly 96; slots at or beyond a device's count are ignored.
All inputs are finite; a program needn't handle non-finite values.
Results may differ from a plain program's by a relative error of at most 0.0009.
The roundings to bfloat16 on the way count: a program that leaves them out, or rounds other values in their place, can miss the bound.
Values may be sent and summed in bfloat16 or wider, within the bound.
A program may use at most 64 MiB of HBM per device.

v0:
```python
import math

import jax
import jax.numpy as jnp
from jax import lax
from jax.sharding import PartitionSpec as P

B = 256
ITERS = 3


def shrink(values):
    return values - jnp.clip(values, -1.0, 1.0)


def local(patch_slots, slot_counts, dictionary):
    slot_rows = patch_slots[0]
    counts = slot_counts[0]
    capacity = slot_rows.shape[0]
    atom_local = dictionary.shape[1]
    atom_count = lax.axis_size("atom")
    atoms_total = atom_local * atom_count
    features = dictionary.shape[0]
    groups = lax.axis_size("dp")
    slot_ends = jnp.cumsum(counts)
    slot_starts = slot_ends - counts
    position = jnp.arange(B, dtype=jnp.int32)
    every_slot = lax.all_gather(slot_rows, "atom", axis=0, tiled=True)
    owner_index = jnp.sum((slot_ends[None, :] <= position[:, None]).astype(jnp.int32), axis=1)
    owner_match = owner_index[:, None] == jnp.arange(counts.shape[0], dtype=jnp.int32)[None, :]
    start_of = jnp.sum(jnp.where(owner_match, slot_starts[None, :], 0), axis=1)
    source = owner_index * capacity + position - start_of
    patches = jnp.take(every_slot, source, axis=0)
    lipschitz = 4.0 * (1.0 + math.sqrt(atoms_total / features)) ** 2
    patch_wide = patches.astype(jnp.float32)
    col_share = features // atom_count

    def residual_of(sparse):
        code_half = sparse.astype(jnp.bfloat16)
        partial_recon = lax.dot_general(
            code_half, dictionary, (((1,), (1,)), ((), ())), preferred_element_type=jnp.float32
        )
        pieces = lax.all_to_all(partial_recon, "atom", split_axis=1, concat_axis=0, tiled=True)
        share = jnp.sum(pieces.reshape(atom_count, B, col_share), axis=0)
        own_cols = lax.dynamic_slice_in_dim(
            patch_wide, lax.axis_index("atom") * col_share, col_share, 1
        )
        res_part = (share / lipschitz - own_cols).astype(jnp.bfloat16)
        residual = lax.all_gather(res_part, "atom", axis=1, tiled=True)
        return (code_half, residual)

    sparse = shrink(jnp.dot(patches, dictionary, preferred_element_type=jnp.float32))
    for step in range(ITERS - 1):
        code_half, residual = residual_of(sparse)
        sparse = shrink(sparse - jnp.dot(residual, dictionary, preferred_element_type=jnp.float32))
    code_half, residual = residual_of(sparse)
    row_share = features // groups
    gradient = lax.psum_scatter(
        lax.dot_general(
            residual, code_half, (((0,), (0,)), ((), ())), preferred_element_type=jnp.float32
        ),
        "dp",
        scatter_dimension=0,
        tiled=True,
    )
    own_rows = lax.dynamic_slice_in_dim(
        dictionary, lax.axis_index("dp") * row_share, row_share, 0
    ).astype(jnp.float32)
    step_norm = 0.5 * math.sqrt(atoms_total)
    grad_total = lax.psum(jnp.sum(gradient * gradient), ("dp", "atom"))
    step_scale = step_norm / jnp.sqrt(grad_total)
    stepped = own_rows - step_scale * gradient
    column_sq = lax.psum(jnp.sum(stepped * stepped, axis=0), "dp")
    new_dictionary = stepped / jnp.sqrt(column_sq + 1e-06)[None, :]
    return (sparse[None], new_dictionary)


def solution(mesh):
    placed = (P("dp", "atom", None), P("dp", None), P(None, "atom"))
    return jax.shard_map(
        local,
        mesh=mesh,
        in_specs=placed,
        out_specs=(P("dp", None, "atom"), P("dp", "atom")),
        check_vma=False,
    )
```

profile of v0, /device:TPU:0, one launch (start us, length us, event | category | flops | bytes accessed | tf_op | source)
XLA Modules:
  0.0 302.1 jit_solution(9952865554270703854)
XLA Ops:
  7.9 0.8 reduce-window.4
  9.6 28.0 %all-gather.3.cloned.1.call-done = bf16[1,768,1024]{2,1,0:T(8,128)(2,1)} async-done(((bf16[1,96,1024]{2,1,0:T(8,128)(2,1)}), bf16[1,768,1024]{2,1,0:T(8,128)(2,1)}) %all-gather.3.cloned.1.call-update) | async-done | bytes 1572880 | tf_op jit(solution)/shard_map/all_gather | solution.py:28
  37.6 3.3 %gather_fusion = bf16[256,1024]{1,0:T(8,128)(2,1)S(1)} fusion(bf16[768,1024]{1,0:T(8,128)(2,1)} %bitcast.38, s32[1024]{0:T(1024)S(1)} %pad_clamp_fusion), kind=kCustom, calls=%fused_computation | custom fusion | bytes 1049600 | tf_op jit(solution)/shard_map/jit(_take)/gather | solution.py:33
  43.4 1.0 copy.19
  44.4 4.2 %all-to-all-start = ((f32[256,8,128]{2,0,1:T(8,128)}), f32[256,8,128]{2,0,1:T(8,128)}, u32[]{:S(2)}, u32[]{:S(2)}) async-start(f32[256,8,128]{2,0,1:T(8,128)} %bitcast.40), calls=%async_computation | async-start | bytes 2097152 | tf_op jit(solution)/shard_map/all_to_all | solution.py:43
  48.7 26.5 %all-to-all-done = f32[256,8,128]{2,0,1:T(8,128)} async-done(((f32[256,8,128]{2,0,1:T(8,128)}), f32[256,8,128]{2,0,1:T(8,128)}, u32[]{:S(2)}, u32[]{:S(2)}) %all-to-all-start) | async-done | bytes 1048608 | tf_op jit(solution)/shard_map/all_to_all | solution.py:43
  75.2 1.3 reduce_sum.68
  76.5 0.9 fusion.10
  77.4 13.9 %all_gather.13 = bf16[256,1024]{1,0:T(8,128)(2,1)S(1)} all-gather(bf16[256,128]{1,0:T(8,128)(2,1)S(1)} %fusion.10), channel_id=1, replica_groups=mesh['dp'=4,'atom'=8] {'atom'}, dimensions={1}, use_global_device_ids=true | all-gather | bytes 589824 | tf_op jit(solution)/shard_map/all_gather | solution.py:49
  93.1 29.0 %all_to_all.39 = f32[256,8,128]{2,0,1:T(8,128)S(1)} all-to-all(f32[256,8,128]{2,0,1:T(8,128)S(1)} %bitcast.41), channel_id=1, replica_groups=mesh['dp'=4,'atom'=8] {'atom'}, dimensions={1} | all-to-all | bytes 2097152 | tf_op jit(solution)/shard_map/all_to_all | solution.py:43
  122.1 0.9 fusion.11
  123.0 13.9 %all_gather.14 = bf16[256,1024]{1,0:T(8,128)(2,1)S(1)} all-gather(bf16[256,128]{1,0:T(8,128)(2,1)S(1)} %fusion.11), channel_id=1, replica_groups=mesh['dp'=4,'atom'=8] {'atom'}, dimensions={1}, use_global_device_ids=true | all-gather | bytes 589824 | tf_op jit(solution)/shard_map/all_gather | solution.py:49
  136.9 1.9 clamp_subtract_fusion
  139.7 29.7 %all_to_all.40 = f32[256,8,128]{2,0,1:T(8,128)} all-to-all(f32[256,8,128]{2,0,1:T(8,128)S(1)} %bitcast.42), channel_id=1, replica_groups=mesh['dp'=4,'atom'=8] {'atom'}, dimensions={1} | all-to-all | bytes 2097152 | tf_op jit(solution)/shard_map/all_to_all | solution.py:43
  169.4 1.3 reduce_sum.70
  170.7 0.9 fusion.9
  171.6 13.9 %all_gather.15 = bf16[256,1024]{1,0:T(8,128)(2,1)S(1)} all-gather(bf16[256,128]{1,0:T(8,128)(2,1)S(1)} %fusion.9), channel_id=1, replica_groups=mesh['dp'=4,'atom'=8] {'atom'}, dimensions={1}, use_global_device_ids=true | all-gather | bytes 589824 | tf_op jit(solution)/shard_map/all_gather | solution.py:49
  185.5 2.7 fusion.6
  188.2 51.2 %reduce-scatter.2.cloned.1.call-done = f32[256,1024]{1,0:T(8,128)} async-done(((f32[1024,1024]{1,0:T(8,128)}), f32[256,1024]{1,0:T(8,128)}) %reduce-scatter.2.cloned.1.call-update) | async-done | bytes 1048592 | tf_op jit(solution)/shard_map/reduce_scatter | solution.py:58
  239.4 2.2 multiply_reduce_fusion.1
  241.6 39.5 %psum.14 = f32[]{:T(128)} all-reduce(f32[]{:T(128)} %multiply_reduce_fusion.1), channel_id=1, replica_groups=mesh['dp'=4,'atom'=8] {'dp','atom'}, use_global_device_ids=true, to_apply=%region_8.9 | all-reduce | flops 1 | bytes 8 | tf_op jit(solution)/shard_map/psum | solution.py:70
  281.8 1.4 multiply_reduce_fusion
  283.2 10.8 %psum.15 = f32[1024]{0:T(1024)S(1)} all-reduce(f32[1024]{0:T(1024)S(1)} %multiply_reduce_fusion), channel_id=1, replica_groups=mesh['dp'=4,'atom'=8] {'dp'}, use_global_device_ids=true, to_apply=%region_10.11 | all-reduce | flops 1024 | bytes 8192 | tf_op jit(solution)/shard_map/psum | solution.py:73
  294.1 1.2 fusion.1
  (31 shorter events, 6.7 us)
Async XLA Ops:
  7.2 30.5 %all-gather.3.cloned.1.call-start = ((), (), s32[]{:S(2)}) async-start(), calls=%async_computation.5 | async-start | bytes 1769472 | tf_op jit(solution)/shard_map/all_gather | solution.py:28
  37.6 4.3 %copy-start = (bf16[1024,1024]{1,0:T(8,128)(2,1)S(1)}, bf16[1024,1024]{1,0:T(8,128)(2,1)}, u32[]{:S(2)}) copy-start(bf16[1024,1024]{1,0:T(8,128)(2,1)} %param.5) | copy-start | bytes 6291460
  41.1 0.8 copy-start.4
  44.4 30.8 %all-to-all-start = ((f32[256,8,128]{2,0,1:T(8,128)}), f32[256,8,128]{2,0,1:T(8,128)}, u32[]{:S(2)}, u32[]{:S(2)}) async-start(f32[256,8,128]{2,0,1:T(8,128)} %bitcast.40), calls=%async_computation | async-start | bytes 2097152 | tf_op jit(solution)/shard_map/all_to_all | solution.py:43
  48.6 190.8 %reduce-scatter.2.cloned.1.call-start = ((), (), s32[]{:S(2)}) async-start(), calls=%async_computation.4 | async-start | bytes 5242880 | tf_op jit(solution)/shard_map/reduce_scatter | solution.py:58
  92.1 1.0 copy-start.3
  138.9 46.6 %copy-start.2 = (f32[256,1024]{1,0:T(8,128)}, f32[256,1024]{1,0:T(8,128)S(1)}, u32[]{:S(2)}) copy-start(f32[256,1024]{1,0:T(8,128)S(1)} %clamp_subtract_fusion) | copy-start | bytes 3145732
  239.4 54.6 %copy-start.1 = (f32[256,1024]{1,0:T(8,128)S(1)}, f32[256,1024]{1,0:T(8,128)}, u32[]{:S(2)}) copy-start(f32[256,1024]{1,0:T(8,128)} %reduce-scatter.2.cloned.1.call-done) | copy-start | bytes 3145732
Sparse Core Ops, SparseCore 0:
  9.6 27.9 all-gather.2
  188.3 51.0 reduce-scatter.1
where the time goes:
time: 303 us; the launch traced here: 302 us
  blocking collectives  151 us (50%)
  waiting for transfers between devices  106 us (35%)
  between operations  14.9 us (5%)
  other arithmetic  11.8 us (4%)
  matrix products  8.33 us (3%)
  local copies, waits for them, and re-layouts  5.5 us (2%)
  starting transfers between devices  4.31 us (1%)
    all_to_all x2, blocking collectives, residual_of(): lax.all_to_all(partial_recon, 'atom', split_axis=1, concat_axis=0, tiled=...  58.6 us
    reduce_scatter x1, waiting for transfers between devices, local(): lax.psum_scatter(lax.dot_general(residual, code_half, (((0,), (0,)), ((),...  51.2 us
    all_gather x3, blocking collectives, residual_of(): residual = lax.all_gather(res_part, 'atom', axis=1, tiled=True)  41.8 us
    psum x1, blocking collectives, local(): grad_total = lax.psum(jnp.sum(gradient * gradient), ('dp', 'atom'))  39.5 us
    all_gather x1, waiting for transfers between devices, local(): every_slot = lax.all_gather(slot_rows, 'atom', axis=0, tiled=True)  28 us
    all_to_all x1, waiting for transfers between devices, residual_of(): lax.all_to_all(partial_recon, 'atom', split_axis=1, concat_axis=0, tiled=...  26.5 us
    psum x1, blocking collectives, local(): column_sq = lax.psum(jnp.sum(stepped * stepped, axis=0), 'dp')  10.8 us
  transfers between devices with their start and end apart: 3, of which 3 were waited for; matrix products, arithmetic and copies ran while one was open for 1% of the time, Pallas kernels for 0%

commit v1 on v0

v1 whole, which is shorter than its diff:
```python
import functools
import math

import jax
import jax.numpy as jnp
from jax import lax
from jax.experimental import pallas as pl
from jax.experimental.pallas import tpu as pltpu
from jax.sharding import PartitionSpec as P

B = 256
ITERS = 3
CORES = 2
LINK = jnp.float32
MESH = pl.DeviceIdType.MESH


def shrink(values):
    return values - jnp.clip(values, -1.0, 1.0)


def kernel(
    groups, chips, counts_ref, slots_ref, dict_ref, codes_ref, newd_ref,
    slots_all, gathered, res, half, sib_send, sib_recv, own_part, z_send, z_recv,
    patch, half_recv, rows_res, grad, tot_send, tot_line, tot_dp, col_send, col_recv,
    send_sem, recv_sem,
):
    atoms_dev = chips * CORES
    capacity, share = slots_ref.shape[1], slots_ref.shape[2]
    features = atoms_dev * share
    atom_local = dict_ref.shape[3]
    atoms_total = atom_local * atoms_dev
    lipschitz = 4.0 * (1.0 + math.sqrt(atoms_total / features)) ** 2
    g = lax.axis_index("dp")
    a = lax.axis_index("atom")
    z, k = a // CORES, a % CORES
    other = 1 - k
    sib = a + 1 - 2 * k
    started = []

    def send(src, dst, device):
        i = len(started)
        copy = pltpu.make_async_remote_copy(
            src_ref=src, dst_ref=dst, send_sem=send_sem.at[i], recv_sem=recv_sem.at[i],
            device_id=device, device_id_type=MESH,
        )
        copy.start()
        started.append(copy)
        return copy

    barrier = pltpu.get_barrier_semaphore()
    for r in range(1, atoms_dev):
        pl.semaphore_signal(barrier, inc=1, device_id=(g, (a + r) % atoms_dev), device_id_type=MESH)
    for q in range(1, groups):
        pl.semaphore_signal(barrier, inc=1, device_id=((g + q) % groups, a), device_id_type=MESH)
    pl.semaphore_wait(barrier, atoms_dev - 1 + groups - 1)

    moves = []
    for r in range(1, atoms_dev):
        peer = (a + r) % atoms_dev
        moves.append(send(slots_ref.at[peer], slots_all.at[a], (g, peer)))
    slots_all[a] = slots_ref[a]
    row = lax.broadcasted_iota(jnp.int32, (capacity, B), 0)
    col = lax.broadcasted_iota(jnp.int32, (capacity, B), 1)
    for c in moves:
        c.wait_recv()
    acc = jnp.zeros((share, B), jnp.float32)
    start = jnp.int32(0)
    for j in range(atoms_dev):
        count = counts_ref[j]
        hit = jnp.logical_and(col - start == row, row < count)
        pick = jnp.where(hit, 1.0, 0.0).astype(jnp.bfloat16)
        acc = acc + lax.dot_general(
            slots_all[j], pick, (((0,), (0,)), ((), ())), preferred_element_type=jnp.float32
        )
        start = start + count
    patch[...] = acc
    gathered[0, a] = (-acc).astype(jnp.bfloat16)

    tile = min(256, atom_local)

    def gather_and_code(t):
        direct = []
        for r in range(1, chips):
            direct.append(send(gathered.at[t, a], gathered.at[t, a], (g, (z + r) % chips * CORES + k)))
        pending = [send(gathered.at[t, a], gathered.at[t, a], (g, sib))]
        for r in range(1, chips):
            direct[r - 1].wait_recv()
            src = (z - r + chips) % chips * CORES + k
            pending.append(send(gathered.at[t, src], gathered.at[t, src], (g, sib)))
        for c in pending:
            c.wait_recv()
        res[...] = gathered[t].reshape(features, B).T

        def body(i, _):
            cols = pl.ds(pl.multiple_of(i * tile, tile), tile)
            d = dict_ref[:, :, :, cols].reshape(features, tile)
            prod = jnp.dot(res[...], d, preferred_element_type=jnp.float32)
            if t == 0:
                new = shrink(-prod)
            else:
                new = shrink(codes_ref[:, cols] - prod)
            codes_ref[:, cols] = new
            half[:, cols] = new.astype(jnp.bfloat16)
            return 0

        lax.fori_loop(0, atom_local // tile, body, 0)

    def partial(core):
        d = dict_ref[:, core].reshape(chips * share, atom_local)
        out = lax.dot_general(
            d, half[...], (((1,), (1,)), ((), ())), preferred_element_type=jnp.float32
        )
        return out.reshape(chips, share, B)

    def residual(t):
        sib_send[t] = partial(other)
        order = list(range(chips - 1, -1, -1))
        moves = {}
        for r in order:
            zz = (z + r) % chips
            moves[r] = send(sib_send.at[t, zz], sib_recv.at[t, zz], (g, sib))
        own_part[...] = partial(k)
        arrivals = []
        mine = None
        for r in order:
            zz = (z + r) % chips
            moves[r].wait_recv()
            both = own_part[zz] + sib_recv[t, zz]
            if r == 0:
                mine = both
            else:
                z_send[t, r - 1] = both.astype(LINK)
                arrivals.append(
                    (r, send(z_send.at[t, r - 1], z_recv.at[t, r - 1], (g, zz * CORES + k)))
                )
        for r, c in arrivals:
            c.wait_recv()
            mine = mine + z_recv[t, r - 1].astype(jnp.float32)
        gathered[t + 1, a] = (mine / lipschitz - patch[...]).astype(jnp.bfloat16)

    for t in range(ITERS - 1):
        gather_and_code(t)
        residual(t)
    gather_and_code(ITERS - 1)
    half_moves = []
    for q in range(1, groups):
        half_moves.append(send(half, half_recv.at[q - 1], ((g + q) % groups, a)))
    residual(ITERS - 1)

    direct = []
    for r in range(1, chips):
        direct.append(
            send(gathered.at[ITERS, a], gathered.at[ITERS, a], (g, (z + r) % chips * CORES + k))
        )
    for c in direct:
        c.wait_recv()
    over = []
    for q in range(1, groups):
        d = (g + q) % groups
        over.append(send(gathered.at[ITERS, d * CORES + k], rows_res.at[g, k], (d, a)))
    rows_res[g, k] = gathered[ITERS, g * CORES + k]
    pending = [send(rows_res.at[g, k], rows_res.at[g, k], (g, sib))]
    for q in range(1, groups):
        over[q - 1].wait_recv()
        src = (g - q + groups) % groups
        pending.append(send(rows_res.at[src, k], rows_res.at[src, k], (g, sib)))
    for q in range(groups):
        pending[q].wait_recv()
        src = (g - q + groups) % groups
        if q > 0:
            half_moves[q - 1].wait_recv()
        left = rows_res[src].reshape(CORES * share, B)
        for i in range(atom_local // tile):
            cols = slice(i * tile, (i + 1) * tile)
            right = half[:, cols] if q == 0 else half_recv[q - 1, :, cols]
            prod = jnp.dot(left, right, preferred_element_type=jnp.float32)
            if q == 0:
                grad[:, cols] = prod
            else:
                grad[:, cols] = grad[:, cols] + prod

    value = grad[...]
    total = jnp.sum(jnp.sum(value * value, axis=0, keepdims=True), axis=1, keepdims=True)
    tot_send[0] = jnp.broadcast_to(total, tot_send.shape[1:])
    moves = []
    for r in range(1, atoms_dev):
        moves.append(send(tot_send.at[0], tot_line.at[r - 1], (g, (a + r) % atoms_dev)))
    line = tot_send[0]
    for r in range(1, atoms_dev):
        moves[r - 1].wait_recv()
        line = line + tot_line[r - 1]
    tot_send[1] = line
    moves = []
    for q in range(1, groups):
        moves.append(send(tot_send.at[1], tot_dp.at[q - 1], ((g + q) % groups, a)))
    for q in range(1, groups):
        moves[q - 1].wait_recv()
        line = line + tot_dp[q - 1]
    scale = (0.5 * math.sqrt(atoms_total)) / jnp.sqrt(line[0:1, 0:1])
    own_rows = dict_ref[g].reshape(CORES * share, atom_local).astype(jnp.float32)
    stepped = own_rows - scale * value
    grad[...] = stepped
    column = jnp.sum(stepped * stepped, axis=0, keepdims=True)
    col_send[...] = jnp.broadcast_to(column, col_send.shape)
    moves = []
    for q in range(1, groups):
        moves.append(send(col_send, col_recv.at[q - 1], ((g + q) % groups, a)))
    for q in range(1, groups):
        moves[q - 1].wait_recv()
        column = column + col_recv[q - 1, 0:1, :]
    newd_ref[...] = grad[...] / jnp.sqrt(column + 1e-06)
    for c in started:
        c.wait_send()


def local(groups, chips, patch_slots, slot_counts, dictionary):
    atoms_dev = chips * CORES
    slots = patch_slots[0]
    capacity, features = slots.shape
    share = features // atoms_dev
    atom_local = dictionary.shape[1]
    slots = slots.reshape(capacity, atoms_dev, share).transpose(1, 0, 2)
    blocks = dictionary.reshape(chips, CORES, share, atom_local)
    rows = CORES * share
    copies = (
        (atoms_dev - 1) + ITERS * (2 * chips - 1) + ITERS * (2 * chips - 1)
        + (groups - 1) + (chips - 1) + (2 * groups - 1) + (atoms_dev - 1) + 2 * (groups - 1)
    )
    bf16, f32 = jnp.bfloat16, jnp.float32
    codes, newd = pl.pallas_call(
        functools.partial(kernel, groups, chips),
        out_shape=(
            jax.ShapeDtypeStruct((B, atom_local), f32),
            jax.ShapeDtypeStruct((rows, atom_local), f32),
        ),
        in_specs=[
            pl.BlockSpec(memory_space=pltpu.SMEM),
            pl.BlockSpec(memory_space=pltpu.VMEM),
            pl.BlockSpec(memory_space=pltpu.VMEM),
        ],
        out_specs=(pl.BlockSpec(memory_space=pltpu.VMEM), pl.BlockSpec(memory_space=pltpu.VMEM)),
        scratch_shapes=[
            pltpu.VMEM((atoms_dev, capacity, share), bf16),
            pltpu.VMEM((ITERS + 1, atoms_dev, share, B), bf16),
            pltpu.VMEM((B, features), bf16),
            pltpu.VMEM((B, atom_local), bf16),
            pltpu.VMEM((ITERS, chips, share, B), f32),
            pltpu.VMEM((ITERS, chips, share, B), f32),
            pltpu.VMEM((chips, share, B), f32),
            pltpu.VMEM((ITERS, chips - 1, share, B), LINK),
            pltpu.VMEM((ITERS, chips - 1, share, B), LINK),
            pltpu.VMEM((share, B), f32),
            pltpu.VMEM((groups - 1, B, atom_local), bf16),
            pltpu.VMEM((groups, CORES, share, B), bf16),
            pltpu.VMEM((rows, atom_local), f32),
            pltpu.VMEM((2, 8, 128), f32),
            pltpu.VMEM((atoms_dev - 1, 8, 128), f32),
            pltpu.VMEM((groups - 1, 8, 128), f32),
            pltpu.VMEM((8, atom_local), f32),
            pltpu.VMEM((groups - 1, 8, atom_local), f32),
            pltpu.SemaphoreType.DMA((copies,)),
            pltpu.SemaphoreType.DMA((copies,)),
        ],
        compiler_params=pltpu.CompilerParams(
            collective_id=0, has_side_effects=True, vmem_limit_bytes=48 * 1024 * 1024
        ),
    )(slot_counts[0], slots, blocks)
    return (codes[None], newd)


def solution(mesh):
    groups = mesh.shape["dp"]
    chips = mesh.shape["atom"] // CORES
    assert chips == groups
    placed = (P("dp", "atom", None), P("dp", None), P(None, "atom"))
    return jax.shard_map(
        functools.partial(local, groups, chips),
        mesh=mesh,
        in_specs=placed,
        out_specs=(P("dp", None, "atom"), P("dp", "atom")),
        check_vma=False,
    )
```

time: 303 us -> 117 us (0.39)
  blocking collectives: 151 us -> 0 us
  Pallas kernels: 0 us -> 111 us
  waiting for transfers between devices: 106 us -> 0 us
  between operations: 14.9 us -> 0.66 us
  other arithmetic: 11.8 us -> 0 us
  matrix products: 8.33 us -> 0 us
  starting transfers between devices: 4.31 us -> 0 us
    pallas_call x0 -> x1, Pallas kernels: none -> 111 us  [local(): pl.pallas_call(functools.partial(kernel, groups, chips), out_shape=(jax.S...]
    all_to_all x2 -> x0, blocking collectives: 58.6 us -> none  [residual_of(): lax.all_to_all(partial_recon, 'atom', split_axis=1, concat_axis=0, tiled=...]
    reduce_scatter x1 -> x0, waiting for transfers between devices: 51.2 us -> none  [local(): lax.psum_scatter(lax.dot_general(residual, code_half, (((0,), (0,)), ((),...]
    psum x2 -> x0, blocking collectives: 50.3 us -> none  [the longest x1 39.5 us: local(): grad_total = lax.psum(jnp.sum(gradient * gradient), ('dp', 'atom'))]
    all_gather x3 -> x0, blocking collectives: 41.8 us -> none  [residual_of(): residual = lax.all_gather(res_part, 'atom', axis=1, tiled=True)]
    all_gather x1 -> x0, waiting for transfers between devices: 28 us -> none  [local(): every_slot = lax.all_gather(slot_rows, 'atom', axis=0, tiled=True)]
    all_to_all x1 -> x0, waiting for transfers between devices: 26.5 us -> none  [residual_of(): lax.all_to_all(partial_recon, 'atom', split_axis=1, concat_axis=0, tiled=...]
    dot_general x7 -> x0, matrix products: 8.33 us -> none  [the longest x1 2.7 us: local(): lax.dot_general(residual, code_half, (((0,), (0,)), ((), ())), preferred_...]
  transfers between devices with their start and end apart: 3 -> 0, of which waited for: 3 -> 0; matrix products, arithmetic and copies ran while one was open for 1% -> 0% of each run, Pallas kernels for 0% -> 0%
where the time goes in v1:
time: 117 us
  Pallas kernels  111 us (95%)
  local copies, waits for them, and re-layouts  5.17 us (4%)
    pallas_call x1, Pallas kernels, local(): pl.pallas_call(functools.partial(kernel, groups, chips), out_shape=(jax.S...  111 us
    unnamed x7, local copies, waits for them, and re-layouts  5.14 us

profile of v1, /device:TPU:0, one launch (start us, length us, event | category | flops | bytes accessed | tf_op | source)
XLA Modules:
  0.0 116.7 jit_solution(11781853810230256273)
XLA Ops:
  0.6 1.0 copy.6
  1.6 0.0 copy-start
  1.6 1.6 %copy-done = bf16[1024,1024]{1,0:T(8,128)(2,1)S(1)} copy-done((bf16[1024,1024]{1,0:T(8,128)(2,1)S(1)}, bf16[1024,1024]{1,0:T(8,128)(2,1)}, u32[]{:S(2)}) %copy-start) | copy-done | bytes 2097176
  3.2 0.0 copy-start.1
  3.2 0.7 copy-done.1
  3.9 110.9 %shard_map.50 = (f32[256,1024]{1,0:T(8,128)S(1)}, f32[256,1024]{1,0:T(8,128)S(1)}) custom-call(s32[8]{0:T(128)S(1)} %bitcast.12, bf16[8,96,128]{2,1,0:T(8,128)(2,1)S(1)} %bitcast.11, bf16[4,2,128,1024]{3,2,1,0:T(8,128)(2,1)S(1)} %bitcast.9), custom_call_target="tpu_custom_call" | custom-call | tf_op jit(solution)/shard_map/pallas_call | solution.py:231
  114.8 1.0 copy.11
  115.7 1.0 copy.12
  (1 shorter events, 0.0 us)
Async XLA Ops:
  1.6 1.6 %copy-start = (bf16[1024,1024]{1,0:T(8,128)(2,1)S(1)}, bf16[1024,1024]{1,0:T(8,128)(2,1)}, u32[]{:S(2)}) copy-start(bf16[1024,1024]{1,0:T(8,128)(2,1)} %param.5) | copy-start | bytes 6291460
  3.2 0.7 copy-start.1

commit v2 on v1

--- a/solution.py
+++ b/solution.py
@@ -11,7 +11,7 @@
 B = 256
 ITERS = 3
 CORES = 2
-LINK = jnp.float32
+LINK = jnp.bfloat16
 MESH = pl.DeviceIdType.MESH
 
 

time: 117 us -> 104 us (0.89)
  Pallas kernels: 111 us -> 98.1 us
    pallas_call x1, Pallas kernels: 111 us -> 98.1 us  [local(): pl.pallas_call(functools.partial(kernel, groups, chips), out_shape=(jax.S...]
where the time goes in v2:
time: 104 us
  Pallas kernels  98.1 us (94%)
  local copies, waits for them, and re-layouts  5.17 us (5%)
    pallas_call x1, Pallas kernels, local(): pl.pallas_call(functools.partial(kernel, groups, chips), out_shape=(jax.S...  98.1 us
    unnamed x7, local copies, waits for them, and re-layouts  5.14 us

profile of v2, /device:TPU:0, one launch (start us, length us, event | category | flops | bytes accessed | tf_op | source)
XLA Modules:
  0.0 104.0 jit_solution(7744404291714882637)
XLA Ops:
  0.6 1.0 copy.6
  1.6 0.0 copy-start
  1.6 1.6 %copy-done = bf16[1024,1024]{1,0:T(8,128)(2,1)S(1)} copy-done((bf16[1024,1024]{1,0:T(8,128)(2,1)S(1)}, bf16[1024,1024]{1,0:T(8,128)(2,1)}, u32[]{:S(2)}) %copy-start) | copy-done | bytes 2097176
  3.2 0.0 copy-start.1
  3.2 0.7 copy-done.1
  3.9 98.1 %shard_map.50 = (f32[256,1024]{1,0:T(8,128)S(1)}, f32[256,1024]{1,0:T(8,128)S(1)}) custom-call(s32[8]{0:T(128)S(1)} %bitcast.12, bf16[8,96,128]{2,1,0:T(8,128)(2,1)S(1)} %bitcast.11, bf16[4,2,128,1024]{3,2,1,0:T(8,128)(2,1)S(1)} %bitcast.9), custom_call_target="tpu_custom_call" | custom-call | tf_op jit(solution)/shard_map/pallas_call | solution.py:231
  102.0 1.0 copy.11
  103.0 1.0 copy.12
  (1 shorter events, 0.0 us)
Async XLA Ops:
  1.6 1.6 %copy-start = (bf16[1024,1024]{1,0:T(8,128)(2,1)S(1)}, bf16[1024,1024]{1,0:T(8,128)(2,1)}, u32[]{:S(2)}) copy-start(bf16[1024,1024]{1,0:T(8,128)(2,1)} %param.5) | copy-start | bytes 6291460
  3.2 0.7 copy-start.1

commit v3 on v2

--- a/solution.py
+++ b/solution.py
@@ -21,7 +21,7 @@
 
 def kernel(
     groups, chips, counts_ref, slots_ref, dict_ref, codes_ref, newd_ref,
-    slots_all, gathered, res, half, sib_send, sib_recv, own_part, z_send, z_recv,
+    slots_all, gathered, res, half, sib_send, sib_recv, own_part, z_send, z_recv, sent_sum, recv_sum,
     patch, half_recv, rows_res, grad, tot_send, tot_line, tot_dp, col_send, col_recv,
     send_sem, recv_sem,
 ):
@@ -112,6 +112,13 @@
             d, half[...], (((1,), (1,)), ((), ())), preferred_element_type=jnp.float32
         )
         return out.reshape(chips, share, B)
+
+    def known(history, t, slot):
+        if t == 0:
+            return jnp.zeros((share, B), jnp.float32)
+        if t == 1:
+            return 2.0 * history[0, slot]
+        return 2.0 * history[t - 1, slot] - history[t - 2, slot]
 
     def residual(t):
         sib_send[t] = partial(other)
@@ -130,13 +137,18 @@
             if r == 0:
                 mine = both
             else:
-                z_send[t, r - 1] = both.astype(LINK)
+                guess = known(sent_sum, t, r - 1)
+                step = (both - guess).astype(LINK)
+                z_send[t, r - 1] = step
+                sent_sum[t, r - 1] = guess + step.astype(jnp.float32)
                 arrivals.append(
                     (r, send(z_send.at[t, r - 1], z_recv.at[t, r - 1], (g, zz * CORES + k)))
                 )
         for r, c in arrivals:
             c.wait_recv()
-            mine = mine + z_recv[t, r - 1].astype(jnp.float32)
+            value = known(recv_sum, t, r - 1) + z_recv[t, r - 1].astype(jnp.float32)
+            recv_sum[t, r - 1] = value
+            mine = mine + value
         gathered[t + 1, a] = (mine / lipschitz - patch[...]).astype(jnp.bfloat16)
 
     for t in range(ITERS - 1):
@@ -250,6 +262,8 @@
             pltpu.VMEM((chips, share, B), f32),
             pltpu.VMEM((ITERS, chips - 1, share, B), LINK),
             pltpu.VMEM((ITERS, chips - 1, share, B), LINK),
+            pltpu.VMEM((ITERS, chips - 1, share, B), f32),
+            pltpu.VMEM((ITERS, chips - 1, share, B), f32),
             pltpu.VMEM((share, B), f32),
             pltpu.VMEM((groups - 1, B, atom_local), bf16),
             pltpu.VMEM((groups, CORES, share, B), bf16),

time: 104 us -> 104 us (level)
  no operation moved by 1% of the time
where the time goes in v3:
time: 104 us
  Pallas kernels  98.1 us (94%)
  local copies, waits for them, and re-layouts  5.17 us (5%)
    pallas_call x1, Pallas kernels, local(): pl.pallas_call(functools.partial(kernel, groups, chips), out_shape=(jax.S...  98.1 us
    unnamed x7, local copies, waits for them, and re-layouts  5.14 us

profile of v3, /device:TPU:0, one launch (start us, length us, event | category | flops | bytes accessed | tf_op | source)
XLA Modules:
  0.0 104.0 jit_solution(167910877457709405)
XLA Ops:
  0.6 1.0 copy.6
  1.6 0.0 copy-start
  1.6 1.6 %copy-done = bf16[1024,1024]{1,0:T(8,128)(2,1)S(1)} copy-done((bf16[1024,1024]{1,0:T(8,128)(2,1)S(1)}, bf16[1024,1024]{1,0:T(8,128)(2,1)}, u32[]{:S(2)}) %copy-start) | copy-done | bytes 2097176
  3.2 0.0 copy-start.1
  3.2 0.7 copy-done.1
  3.9 98.1 %shard_map.50 = (f32[256,1024]{1,0:T(8,128)S(1)}, f32[256,1024]{1,0:T(8,128)S(1)}) custom-call(s32[8]{0:T(128)S(1)} %bitcast.12, bf16[8,96,128]{2,1,0:T(8,128)(2,1)S(1)} %bitcast.11, bf16[4,2,128,1024]{3,2,1,0:T(8,128)(2,1)S(1)} %bitcast.9), custom_call_target="tpu_custom_call" | custom-call | tf_op jit(solution)/shard_map/pallas_call | solution.py:243
  102.0 1.0 copy.11
  103.0 1.0 copy.12
  (1 shorter events, 0.0 us)
Async XLA Ops:
  1.6 1.6 %copy-start = (bf16[1024,1024]{1,0:T(8,128)(2,1)S(1)}, bf16[1024,1024]{1,0:T(8,128)(2,1)}, u32[]{:S(2)}) copy-start(bf16[1024,1024]{1,0:T(8,128)(2,1)} %param.5) | copy-start | bytes 6291460
  3.2 0.7 copy-start.1

commit v4 on v2

--- a/solution.py
+++ b/solution.py
@@ -11,6 +11,7 @@
 B = 256
 ITERS = 3
 CORES = 2
+PARTS = 2
 LINK = jnp.bfloat16
 MESH = pl.DeviceIdType.MESH
 
@@ -21,7 +22,7 @@
 
 def kernel(
     groups, chips, counts_ref, slots_ref, dict_ref, codes_ref, newd_ref,
-    slots_all, gathered, res, half, sib_send, sib_recv, own_part, z_send, z_recv,
+    slots_all, gathered, res, half, sib_send, sib_recv, own_part, z_send, z_recv, sent_sum, recv_sum,
     patch, half_recv, rows_res, grad, tot_send, tot_line, tot_dp, col_send, col_recv,
     send_sem, recv_sem,
 ):
@@ -37,6 +38,7 @@
     other = 1 - k
     sib = a + 1 - 2 * k
     started = []
+    span = B // PARTS
 
     def send(src, dst, device):
         i = len(started)
@@ -74,107 +76,163 @@
             slots_all[j], pick, (((0,), (0,)), ((), ())), preferred_element_type=jnp.float32
         )
         start = start + count
-    patch[...] = acc
-    gathered[0, a] = (-acc).astype(jnp.bfloat16)
 
     tile = min(256, atom_local)
-
-    def gather_and_code(t):
-        direct = []
-        for r in range(1, chips):
-            direct.append(send(gathered.at[t, a], gathered.at[t, a], (g, (z + r) % chips * CORES + k)))
-        pending = [send(gathered.at[t, a], gathered.at[t, a], (g, sib))]
+    tiles = atom_local // tile
+
+    def along(t, h):
+        return [
+            send(gathered.at[t, h, a], gathered.at[t, h, a], (g, (z + r) % chips * CORES + k))
+            for r in range(1, chips)
+        ]
+
+    def gather_start(t, h):
+        direct = along(t, h)
+        return direct, [send(gathered.at[t, h, a], gathered.at[t, h, a], (g, sib))]
+
+    def gather_end(t, h, direct, pending):
         for r in range(1, chips):
             direct[r - 1].wait_recv()
             src = (z - r + chips) % chips * CORES + k
-            pending.append(send(gathered.at[t, src], gathered.at[t, src], (g, sib)))
+            pending.append(send(gathered.at[t, h, src], gathered.at[t, h, src], (g, sib)))
         for c in pending:
             c.wait_recv()
-        res[...] = gathered[t].reshape(features, B).T
+
+    def code(t, h):
+        res[h] = gathered[t, h].reshape(features, span).T
+        rows = slice(h * span, (h + 1) * span)
 
         def body(i, _):
             cols = pl.ds(pl.multiple_of(i * tile, tile), tile)
             d = dict_ref[:, :, :, cols].reshape(features, tile)
-            prod = jnp.dot(res[...], d, preferred_element_type=jnp.float32)
+            prod = jnp.dot(res[h], d, preferred_element_type=jnp.float32)
             if t == 0:
                 new = shrink(-prod)
             else:
-                new = shrink(codes_ref[:, cols] - prod)
-            codes_ref[:, cols] = new
-            half[:, cols] = new.astype(jnp.bfloat16)
+                new = shrink(codes_ref[rows, cols] - prod)
+            codes_ref[rows, cols] = new
+            half[h, :, cols] = new.astype(jnp.bfloat16)
             return 0
 
-        lax.fori_loop(0, atom_local // tile, body, 0)
-
-    def partial(core):
+        lax.fori_loop(0, tiles, body, 0)
+
+    def partial(h, core):
         d = dict_ref[:, core].reshape(chips * share, atom_local)
         out = lax.dot_general(
-            d, half[...], (((1,), (1,)), ((), ())), preferred_element_type=jnp.float32
+            d, half[h], (((1,), (1,)), ((), ())), preferred_element_type=jnp.float32
         )
-        return out.reshape(chips, share, B)
-
-    def residual(t):
-        sib_send[t] = partial(other)
-        order = list(range(chips - 1, -1, -1))
+        return out.reshape(chips, share, span)
+
+    def known(history, t, h, slot):
+        if t == 1:
+            return 2.0 * history[0, h, slot]
+        return 2.0 * history[t - 1, h, slot] - history[t - 2, h, slot]
+
+    order = list(range(chips - 1, -1, -1))
+
+    def recon_start(t, h):
+        sib_send[t, h] = partial(h, other)
         moves = {}
         for r in order:
             zz = (z + r) % chips
-            moves[r] = send(sib_send.at[t, zz], sib_recv.at[t, zz], (g, sib))
-        own_part[...] = partial(k)
+            moves[r] = send(sib_send.at[t, h, zz], sib_recv.at[t, h, zz], (g, sib))
+        own_part[h] = partial(h, k)
+        return moves
+
+    def recon_mid(t, h, moves):
         arrivals = []
         mine = None
         for r in order:
             zz = (z + r) % chips
             moves[r].wait_recv()
-            both = own_part[zz] + sib_recv[t, zz]
+            both = own_part[h, zz] + sib_recv[t, h, zz]
             if r == 0:
                 mine = both
+                continue
+            dest = zz * CORES + k
+            s = r - 1
+            if t == 0:
+                base = gathered[0, h, dest].astype(jnp.float32)
+                fit = jnp.sum(both * base, axis=0, keepdims=True)
+                fit = fit / (jnp.sum(base * base, axis=0, keepdims=True) + 1e-30)
+                fit = fit.astype(LINK)
+                z_send[t, h, s, share:] = jnp.broadcast_to(fit, (16, span))
+                guess = fit.astype(jnp.float32) * base
+                rows = share + 16
             else:
-                z_send[t, r - 1] = both.astype(LINK)
-                arrivals.append(
-                    (r, send(z_send.at[t, r - 1], z_recv.at[t, r - 1], (g, zz * CORES + k)))
-                )
-        for r, c in arrivals:
+                guess = known(sent_sum, t, h, s)
+                rows = share
+            step = (both - guess).astype(LINK)
+            z_send[t, h, s, :share] = step
+            sent_sum[t, h, s] = guess + step.astype(jnp.float32)
+            arrivals.append(
+                (s, send(z_send.at[t, h, s, pl.ds(0, rows)], z_recv.at[t, h, s, pl.ds(0, rows)], (g, dest)))
+            )
+        return mine, arrivals
+
+    def recon_end(t, h, mine, arrivals):
+        for s, c in arrivals:
             c.wait_recv()
-            mine = mine + z_recv[t, r - 1].astype(jnp.float32)
-        gathered[t + 1, a] = (mine / lipschitz - patch[...]).astype(jnp.bfloat16)
-
-    for t in range(ITERS - 1):
-        gather_and_code(t)
-        residual(t)
-    gather_and_code(ITERS - 1)
+            if t == 0:
+                guess = z_recv[t, h, s, share:share + 1].astype(jnp.float32) * (-patch[h])
+            else:
+                guess = known(recv_sum, t, h, s)
+            value = guess + z_recv[t, h, s, :share].astype(jnp.float32)
+            recv_sum[t, h, s] = value
+            mine = mine + value
+        gathered[t + 1, h, a] = (mine / lipschitz - patch[h]).astype(jnp.bfloat16)
+
+    gathers = []
+    for h in range(PARTS):
+        patch[h] = acc[:, h * span:(h + 1) * span]
+        gathered[0, h, a] = (-patch[h]).astype(jnp.bfloat16)
+        gathers.append(gather_start(0, h))
     half_moves = []
-    for q in range(1, groups):
-        half_moves.append(send(half, half_recv.at[q - 1], ((g + q) % groups, a)))
-    residual(ITERS - 1)
-
-    direct = []
-    for r in range(1, chips):
-        direct.append(
-            send(gathered.at[ITERS, a], gathered.at[ITERS, a], (g, (z + r) % chips * CORES + k))
+    for t in range(ITERS):
+        last = t == ITERS - 1
+        starts, mids = [], []
+        for h in range(PARTS):
+            gather_end(t, h, *gathers[h])
+            if h > 0:
+                mids.append(recon_mid(t, h - 1, starts[h - 1]))
+            code(t, h)
+            if last:
+                for q in range(1, groups):
+                    half_moves.append(
+                        send(half.at[h], half_recv.at[q - 1, h], ((g + q) % groups, a))
+                    )
+            starts.append(recon_start(t, h))
+        mids.append(recon_mid(t, PARTS - 1, starts[PARTS - 1]))
+        gathers = []
+        for h in range(PARTS):
+            recon_end(t, h, *mids[h])
+            gathers.append(along(t + 1, h) if last else gather_start(t + 1, h))
+
+    over, pending = [], []
+    for h in range(PARTS):
+        for c in gathers[h]:
+            c.wait_recv()
+        for q in range(1, groups):
+            d = (g + q) % groups
+            over.append(send(gathered.at[ITERS, h, d * CORES + k], rows_res.at[g, h, k], (d, a)))
+        rows_res[g, h, k] = gathered[ITERS, h, g * CORES + k]
+        pending.append(send(rows_res.at[g, h, k], rows_res.at[g, h, k], (g, sib)))
+    for h in range(PARTS):
+        for q in range(1, groups):
+            over[h * (groups - 1) + q - 1].wait_recv()
+            src = (g - q + groups) % groups
+            pending.append(send(rows_res.at[src, h, k], rows_res.at[src, h, k], (g, sib)))
+    for c in pending + half_moves:
+        c.wait_recv()
+    for q in range(groups):
+        src = (g - q + groups) % groups
+        left = jnp.concatenate(
+            [rows_res[src, h].reshape(CORES * share, span) for h in range(PARTS)], axis=1
         )
-    for c in direct:
-        c.wait_recv()
-    over = []
-    for q in range(1, groups):
-        d = (g + q) % groups
-        over.append(send(gathered.at[ITERS, d * CORES + k], rows_res.at[g, k], (d, a)))
-    rows_res[g, k] = gathered[ITERS, g * CORES + k]
-    pending = [send(rows_res.at[g, k], rows_res.at[g, k], (g, sib))]
-    for q in range(1, groups):
-        over[q - 1].wait_recv()
-        src = (g - q + groups) % groups
-        pending.append(send(rows_res.at[src, k], rows_res.at[src, k], (g, sib)))
-    for q in range(groups):
-        pending[q].wait_recv()
-        src = (g - q + groups) % groups
-        if q > 0:
-            half_moves[q - 1].wait_recv()
-        left = rows_res[src].reshape(CORES * share, B)
-        for i in range(atom_local // tile):
+        for i in range(tiles):
             cols = slice(i * tile, (i + 1) * tile)
-            right = half[:, cols] if q == 0 else half_recv[q - 1, :, cols]
-            prod = jnp.dot(left, right, preferred_element_type=jnp.float32)
+            right = half[:, :, cols] if q == 0 else half_recv[q - 1, :, :, cols]
+            prod = jnp.dot(left, right.reshape(B, tile), preferred_element_type=jnp.float32)
             if q == 0:
                 grad[:, cols] = prod
             else:
@@ -224,9 +282,10 @@
     blocks = dictionary.reshape(chips, CORES, share, atom_local)
     rows = CORES * share
     copies = (
-        (atoms_dev - 1) + ITERS * (2 * chips - 1) + ITERS * (2 * chips - 1)
-        + (groups - 1) + (chips - 1) + (2 * groups - 1) + (atoms_dev - 1) + 2 * (groups - 1)
+        2 * (atoms_dev - 1) + 2 * (groups - 1)
+        + PARTS * (2 * ITERS * (2 * chips - 1) + (chips - 1) + (groups - 1) + (2 * groups - 1))
     )
+    span = B // PARTS
     bf16, f32 = jnp.bfloat16, jnp.float32
     codes, newd = pl.pallas_call(
         functools.partial(kernel, groups, chips),
@@ -242,17 +301,19 @@
         out_specs=(pl.BlockSpec(memory_space=pltpu.VMEM), pl.BlockSpec(memory_space=pltpu.VMEM)),
         scratch_shapes=[
             pltpu.VMEM((atoms_dev, capacity, share), bf16),
-            pltpu.VMEM((ITERS + 1, atoms_dev, share, B), bf16),
-            pltpu.VMEM((B, features), bf16),
-            pltpu.VMEM((B, atom_local), bf16),
-            pltpu.VMEM((ITERS, chips, share, B), f32),
-            pltpu.VMEM((ITERS, chips, share, B), f32),
-            pltpu.VMEM((chips, share, B), f32),
-            pltpu.VMEM((ITERS, chips - 1, share, B), LINK),
-            pltpu.VMEM((ITERS, chips - 1, share, B), LINK),
-            pltpu.VMEM((share, B), f32),
-            pltpu.VMEM((groups - 1, B, atom_local), bf16),
-            pltpu.VMEM((groups, CORES, share, B), bf16),
+            pltpu.VMEM((ITERS + 1, PARTS, atoms_dev, share, span), bf16),
+            pltpu.VMEM((PARTS, span, features), bf16),
+            pltpu.VMEM((PARTS, span, atom_local), bf16),
+            pltpu.VMEM((ITERS, PARTS, chips, share, span), f32),
+            pltpu.VMEM((ITERS, PARTS, chips, share, span), f32),
+            pltpu.VMEM((PARTS, chips, share, span), f32),
+            pltpu.VMEM((ITERS, PARTS, chips - 1, share + 16, span), LINK),
+            pltpu.VMEM((ITERS, PARTS, chips - 1, share + 16, span), LINK),
+            pltpu.VMEM((ITERS, PARTS, chips - 1, share, span), f32),
+            pltpu.VMEM((ITERS, PARTS, chips - 1, share, span), f32),
+            pltpu.VMEM((PARTS, share, span), f32),
+            pltpu.VMEM((groups - 1, PARTS, span, atom_local), bf16),
+            pltpu.VMEM((groups, PARTS, CORES, share, span), bf16),
             pltpu.VMEM((rows, atom_local), f32),
             pltpu.VMEM((2, 8, 128), f32),
             pltpu.VMEM((atoms_dev - 1, 8, 128), f32),

time: 104 us -> 99.8 us (0.960)
  Pallas kernels: 98.1 us -> 93.7 us
    pallas_call x1, Pallas kernels: 98.1 us -> 93.7 us  [local(): pl.pallas_call(functools.partial(kernel, groups, chips), out_shape=(jax.S...]
where the time goes in v4:
time: 99.8 us; the launch traced here: 99.6 us
  Pallas kernels  93.7 us (94%)
  local copies, waits for them, and re-layouts  5.17 us (5%)
    pallas_call x1, Pallas kernels, local(): pl.pallas_call(functools.partial(kernel, groups, chips), out_shape=(jax.S...  93.7 us
    unnamed x7, local copies, waits for them, and re-layouts  5.14 us

profile of v4, /device:TPU:0, one launch (start us, length us, event | category | flops | bytes accessed | tf_op | source)
XLA Modules:
  0.0 99.6 jit_solution(9770657225802715065)
XLA Ops:
  0.6 1.0 copy.6
  1.6 0.0 copy-start
  1.6 1.6 %copy-done = bf16[1024,1024]{1,0:T(8,128)(2,1)S(1)} copy-done((bf16[1024,1024]{1,0:T(8,128)(2,1)S(1)}, bf16[1024,1024]{1,0:T(8,128)(2,1)}, u32[]{:S(2)}) %copy-start) | copy-done | bytes 2097176
  3.2 0.0 copy-start.1
  3.2 0.7 copy-done.1
  3.9 93.7 %shard_map.50 = (f32[256,1024]{1,0:T(8,128)S(1)}, f32[256,1024]{1,0:T(8,128)S(1)}) custom-call(s32[8]{0:T(128)S(1)} %bitcast.12, bf16[8,96,128]{2,1,0:T(8,128)(2,1)S(1)} %bitcast.11, bf16[4,2,128,1024]{3,2,1,0:T(8,128)(2,1)S(1)} %bitcast.9), custom_call_target="tpu_custom_call" | custom-call | tf_op jit(solution)/shard_map/pallas_call | solution.py:290
  97.6 1.0 copy.11
  98.6 1.0 copy.12
  (1 shorter events, 0.0 us)
Async XLA Ops:
  1.6 1.6 %copy-start = (bf16[1024,1024]{1,0:T(8,128)(2,1)S(1)}, bf16[1024,1024]{1,0:T(8,128)(2,1)}, u32[]{:S(2)}) copy-start(bf16[1024,1024]{1,0:T(8,128)(2,1)} %param.5) | copy-start | bytes 6291460
  3.2 0.7 copy-start.1

commit v5 on v4

--- a/solution.py
+++ b/solution.py
@@ -21,13 +21,13 @@
 
 
 def kernel(
-    groups, chips, counts_ref, slots_ref, dict_ref, codes_ref, newd_ref,
+    groups, chips, counts_ref, slots_ref, dict_hbm, codes_hbm, newd_ref, dict_ref, codes_ref,
     slots_all, gathered, res, half, sib_send, sib_recv, own_part, z_send, z_recv, sent_sum, recv_sum,
     patch, half_recv, rows_res, grad, tot_send, tot_line, tot_dp, col_send, col_recv,
-    send_sem, recv_sem,
+    send_sem, recv_sem, load_sem,
 ):
     atoms_dev = chips * CORES
-    capacity, share = slots_ref.shape[1], slots_ref.shape[2]
+    capacity, share = slots_all.shape[1], slots_all.shape[2]
     features = atoms_dev * share
     atom_local = dict_ref.shape[3]
     atoms_total = atom_local * atoms_dev
@@ -50,6 +50,16 @@
         started.append(copy)
         return copy
 
+    load = pltpu.make_async_copy(dict_hbm, dict_ref, load_sem.at[0])
+    load.start()
+
+    def slots_of(device):
+        if share % 128:
+            return slots_ref.at[device]
+        return slots_ref.at[:, pl.ds(pl.multiple_of(device * share, share), share)]
+
+    keep = pltpu.make_async_copy(slots_of(a), slots_all.at[a], load_sem.at[1])
+    keep.start()
     barrier = pltpu.get_barrier_semaphore()
     for r in range(1, atoms_dev):
         pl.semaphore_signal(barrier, inc=1, device_id=(g, (a + r) % atoms_dev), device_id_type=MESH)
@@ -60,12 +70,12 @@
     moves = []
     for r in range(1, atoms_dev):
         peer = (a + r) % atoms_dev
-        moves.append(send(slots_ref.at[peer], slots_all.at[a], (g, peer)))
-    slots_all[a] = slots_ref[a]
+        moves.append(send(slots_of(peer), slots_all.at[a], (g, peer)))
     row = lax.broadcasted_iota(jnp.int32, (capacity, B), 0)
     col = lax.broadcasted_iota(jnp.int32, (capacity, B), 1)
     for c in moves:
         c.wait_recv()
+    keep.wait()
     acc = jnp.zeros((share, B), jnp.float32)
     start = jnp.int32(0)
     for j in range(atoms_dev):
@@ -182,12 +192,24 @@
             mine = mine + value
         gathered[t + 1, h, a] = (mine / lipschitz - patch[h]).astype(jnp.bfloat16)
 
+    load.wait()
     gathers = []
     for h in range(PARTS):
         patch[h] = acc[:, h * span:(h + 1) * span]
         gathered[0, h, a] = (-patch[h]).astype(jnp.bfloat16)
         gathers.append(gather_start(0, h))
     half_moves = []
+    square = groups == 4 and PARTS == 2
+    near = [g // 2 * 2 + 1 - g % 2, (g + 2) % 4]
+    sources = near + [(near[0] + 2) % 4]
+
+    def relay(h):
+        came, onward = (1, 0) if h == 0 else (0, 1)
+        half_moves[2 * h + came].wait_recv()
+        taken.add(2 * h + came)
+        relayed.append(send(half_recv.at[came, h], half_recv.at[2, h], (near[onward], a)))
+
+    taken, relayed, stores = set(), [], []
     for t in range(ITERS):
         last = t == ITERS - 1
         starts, mids = [], []
@@ -197,17 +219,31 @@
                 mids.append(recon_mid(t, h - 1, starts[h - 1]))
             code(t, h)
             if last:
+                rows = pl.ds(h * span, span)
+                store = pltpu.make_async_copy(
+                    codes_ref.at[rows], codes_hbm.at[rows], load_sem.at[2 + h]
+                )
+                store.start()
+                stores.append(store)
+            if last and square:
+                for q in range(2):
+                    half_moves.append(send(half.at[h], half_recv.at[q, h], (near[q], a)))
+            elif last:
                 for q in range(1, groups):
                     half_moves.append(
                         send(half.at[h], half_recv.at[q - 1, h], ((g + q) % groups, a))
                     )
             starts.append(recon_start(t, h))
         mids.append(recon_mid(t, PARTS - 1, starts[PARTS - 1]))
+        if last and square:
+            relay(0)
         gathers = []
         for h in range(PARTS):
             recon_end(t, h, *mids[h])
             gathers.append(along(t + 1, h) if last else gather_start(t + 1, h))
 
+    if square:
+        relay(1)
     over, pending = [], []
     for h in range(PARTS):
         for c in gathers[h]:
@@ -222,10 +258,14 @@
             over[h * (groups - 1) + q - 1].wait_recv()
             src = (g - q + groups) % groups
             pending.append(send(rows_res.at[src, h, k], rows_res.at[src, h, k], (g, sib)))
-    for c in pending + half_moves:
+    rest = [c for i, c in enumerate(half_moves) if i not in taken]
+    for c in pending + rest + relayed:
         c.wait_recv()
     for q in range(groups):
-        src = (g - q + groups) % groups
+        if square and q:
+            src = sources[q - 1]
+        else:
+            src = (g - q + groups) % groups
         left = jnp.concatenate(
             [rows_res[src, h].reshape(CORES * share, span) for h in range(PARTS)], axis=1
         )
@@ -268,6 +308,8 @@
         moves[q - 1].wait_recv()
         column = column + col_recv[q - 1, 0:1, :]
     newd_ref[...] = grad[...] / jnp.sqrt(column + 1e-06)
+    for c in stores:
+        c.wait()
     for c in started:
         c.wait_send()
 
@@ -278,7 +320,8 @@
     capacity, features = slots.shape
     share = features // atoms_dev
     atom_local = dictionary.shape[1]
-    slots = slots.reshape(capacity, atoms_dev, share).transpose(1, 0, 2)
+    if share % 128:
+        slots = slots.reshape(capacity, atoms_dev, share).transpose(1, 0, 2)
     blocks = dictionary.reshape(chips, CORES, share, atom_local)
     rows = CORES * share
     copies = (
@@ -295,11 +338,13 @@
         ),
         in_specs=[
             pl.BlockSpec(memory_space=pltpu.SMEM),
-            pl.BlockSpec(memory_space=pltpu.VMEM),
-            pl.BlockSpec(memory_space=pltpu.VMEM),
+            pl.BlockSpec(memory_space=pl.ANY),
+            pl.BlockSpec(memory_space=pl.ANY),
         ],
-        out_specs=(pl.BlockSpec(memory_space=pltpu.VMEM), pl.BlockSpec(memory_space=pltpu.VMEM)),
+        out_specs=(pl.BlockSpec(memory_space=pl.ANY), pl.BlockSpec(memory_space=pltpu.VMEM)),
         scratch_shapes=[
+            pltpu.VMEM((chips, CORES, share, atom_local), bf16),
+            pltpu.VMEM((B, atom_local), f32),
             pltpu.VMEM((atoms_dev, capacity, share), bf16),
             pltpu.VMEM((ITERS + 1, PARTS, atoms_dev, share, span), bf16),
             pltpu.VMEM((PARTS, span, features), bf16),
@@ -322,9 +367,10 @@
             pltpu.VMEM((groups - 1, 8, atom_local), f32),
             pltpu.SemaphoreType.DMA((copies,)),
             pltpu.SemaphoreType.DMA((copies,)),
+            pltpu.SemaphoreType.DMA((2 + PARTS,)),
         ],
         compiler_params=pltpu.CompilerParams(
-            collective_id=0, has_side_effects=True, vmem_limit_bytes=48 * 1024 * 1024
+            collective_id=0, has_side_effects=True, vmem_limit_bytes=62 * 1024 * 1024
         ),
     )(slot_counts[0], slots, blocks)
     return (codes[None], newd)

time: 99.8 us -> 95.5 us (0.957)
  Pallas kernels: 93.7 us -> 91.3 us
  local copies, waits for them, and re-layouts: 5.17 us -> 3.37 us
    pallas_call x1, Pallas kernels: 93.7 us -> 91.3 us  [local(): pl.pallas_call(functools.partial(kernel, groups, chips), out_shape=(jax.S...]
    unnamed x7 -> x4, local copies, waits for them, and re-layouts: 5.14 us -> 3.37 us
where the time goes in v5:
time: 95.5 us; the launch traced here: 95.3 us
  Pallas kernels  91.3 us (96%)
  local copies, waits for them, and re-layouts  3.37 us (4%)
    pallas_call x1, Pallas kernels, local(): pl.pallas_call(functools.partial(kernel, groups, chips), out_shape=(jax.S...  91.3 us
    unnamed x4, local copies, waits for them, and re-layouts  3.37 us

profile of v5, /device:TPU:0, one launch (start us, length us, event | category | flops | bytes accessed | tf_op | source)
XLA Modules:
  0.0 95.3 jit_solution(5476707561781794981)
XLA Ops:
  0.6 91.3 %shard_map.50 = (f32[256,1024]{1,0:T(8,128)}, f32[256,1024]{1,0:T(8,128)}) custom-call(s32[8]{0:T(128)} %bitcast.7, bf16[96,1024]{1,0:T(8,128)(2,1)} %bitcast.6, bf16[4,2,128,1024]{3,2,1,0:T(8,128)(2,1)} %bitcast.4), custom_call_target="tpu_custom_call" | custom-call | tf_op jit(solution)/shard_map/pallas_call | solution.py:333
  92.0 0.0 copy-start
  92.0 2.4 %copy.7 = f32[1,256,1024]{2,1,0:T(8,128)} copy(f32[1,256,1024]{2,1,0:T(8,128)} %bitcast.5) | data formatting | bytes 2097152
  94.4 0.0 copy-done
  94.4 1.0 %copy.8 = f32[256,1024]{1,0:T(8,128)} copy(f32[256,1024]{1,0:T(8,128)S(1)} %copy-done) | data formatting | bytes 2097152
Async XLA Ops:
  92.0 2.4 %copy-start = (f32[256,1024]{1,0:T(8,128)S(1)}, f32[256,1024]{1,0:T(8,128)}, u32[]{:S(2)}) copy-start(f32[256,1024]{1,0:T(8,128)} %get-tuple-element.9) | copy-start | bytes 3145732
